TPU v7x, 32 devices: a whole 2x2x4 slice. The times are simulated.
32 devices in a mesh: dp: 2 (over core), seq: 16 (over z, y, x).
Axes of the slice: x: 2, y: 2, z: 4, core: 2. Of those that a mesh axis runs over, the one named last changes fastest.
Arguments:
- tokens: bfloat16 [32768, 768], P(('dp', 'seq')), may hold values from -6 to 6
- doc_start: int32 [32768], P(('dp', 'seq')), may hold values from 0 to 32767, as said below
- real: int32 [32768], P(('dp', 'seq')), may hold values from 0 to 1, as said below
- w_qkv: bfloat16 [768, 2304], P('dp', 'seq'), may hold values from -0.3125 to 0.3125
- w_out: bfloat16 [768, 768], P('dp', 'seq'), may hold values from -1 to 1
- w_in: bfloat16 [768, 2304], P('dp', 'seq'), may hold values from -0.21875 to 0.21875
- w_down: bfloat16 [1152, 768], P('dp', 'seq'), may hold values from -0.375 to 0.375
- gain_attn: bfloat16 [768], P('seq'), may hold values from 0.5 to 1.5
- gain_mlp: bfloat16 [768], P('seq'), may hold values from 0.5 to 1.5
- cotangent: bfloat16 [32768, 768], P(('dp', 'seq')), may hold values from -6 to 6
Outputs:
- output: bfloat16 [32768, 768], P(('dp', 'seq'))
- grad_tokens: float32 [32768, 768], P(('dp', 'seq'))
- grad_w_qkv: float32 [768, 2304], P('dp', 'seq')
- grad_w_out: float32 [768, 768], P('dp', 'seq')
- grad_w_in: float32 [768, 2304], P('dp', 'seq')
- grad_w_down: float32 [1152, 768], P('dp', 'seq')
- grad_gain_attn: float32 [768], P('seq')
- grad_gain_mlp: float32 [768], P('seq')
Inputs may be any that keep to these rules, and one draw needn't show every extreme that they name: `doc_start`: for each slot, the index in the whole stream of 32768 slots of the first slot of its document; packed rows begin at slots 8192 / 2 + k * 8192, so the first and the last row hold 4096 slots and the others 8192; documents never cross a row, and a row's padding forms a document of its own. `real`: each packed row ends in one or more padding slots and has no others.
All inputs are finite; a program needn't handle non-finite values.
Results may differ from a plain program's by a relative error of at most 0.014.
The roundings to bfloat16 on the way count: a program that leaves them out, or rounds other values in their place, can miss the bound.
Values may be sent and summed in bfloat16 or wider, within the bound.
A program may use at most 192 MiB of HBM per device.

v0:
```python
import functools
import math

import jax
import jax.numpy as jnp
from jax import lax
from jax.experimental import pallas as pl
from jax.experimental.pallas import tpu as pltpu
from jax.sharding import PartitionSpec as P

D = 768
HEADS = 12
HEAD = 64
FF = 1152
HALF = 64


def padded(value, sides, width):
    for axis, dim in sides:
        size, length = (lax.axis_size(axis), value.shape[dim])
        up = [(i, (i + 1) % size) for i in range(size - 1)]
        down = [(j, i) for i, j in up]
        last = lax.slice_in_dim(value, length - width, length, axis=dim)
        initial = lax.slice_in_dim(value, 0, width, axis=dim)
        before = lax.ppermute(last, axis, up)
        after = lax.ppermute(initial, axis, down)
        value = jnp.concatenate([before, value, after], axis=dim)
    return value


def shifted(value, axis, by):
    length = lax.axis_size(axis)
    pairs = [(i, i + by) for i in range(length) if 0 <= i + by < length]
    return lax.ppermute(value, axis, pairs)


def layer_norm(value):
    centre = value - jnp.mean(value, axis=-1, keepdims=True)
    factor = lax.rsqrt(jnp.mean(centre * centre, axis=-1, keepdims=True) + 1e-05)
    return (centre * factor, factor)


def norm_back(grad, normed, factor):
    return factor * (
        grad
        - jnp.mean(grad, axis=-1, keepdims=True)
        - normed * jnp.mean(grad * normed, axis=-1, keepdims=True)
    )


def rotary_tables(place):
    freq = jnp.exp(jnp.arange(HEAD // 2, dtype=jnp.float32) * (-2.0 * math.log(10000.0) / HEAD))
    angle = place[:, None] * freq[None, :]
    cosine = jnp.tile(jnp.concatenate([jnp.cos(angle), jnp.cos(angle)], 1), (1, HEADS))
    sine = jnp.tile(jnp.concatenate([jnp.sin(angle), jnp.sin(angle)], 1), (1, HEADS))
    return (cosine, sine)


def rotate(value):
    count = value.shape[0]
    shaped = value.reshape(count, HEADS, HEAD)
    first = shaped[..., : HEAD // 2]
    second = shaped[..., HEAD // 2 :]
    return jnp.concatenate([-second, first], -1).reshape(count, HEADS * HEAD)


def left_dot(left, right):
    return lax.dot_general(
        left, right, (((0,), (0,)), ((), ())), preferred_element_type=jnp.float32
    )


def right_dot(left, right):
    return lax.dot_general(
        left, right, (((1,), (1,)), ((), ())), preferred_element_type=jnp.float32
    )


def glu_piece(gate_up):
    return jax.nn.gelu(gate_up[:, :FF], approximate=False) * gate_up[:, FF:]


MESH = pl.DeviceIdType.MESH


def ring_order(mesh):
    n = mesh.shape["seq"]
    try:
        coords = [tuple(mesh.devices[0, s].coords) for s in range(n)]
    except Exception:
        return list(range(n))
    near = [
        [t for t in range(n) if sum(abs(a - b) for a, b in zip(coords[s], coords[t])) == 1]
        for s in range(n)
    ]
    path, seen = [0], {0}

    def grow(budget=[200000]):
        budget[0] -= 1
        if budget[0] < 0:
            return False
        if len(path) == n:
            return 0 in near[path[-1]]
        options = sorted(
            (t for t in near[path[-1]] if t not in seen),
            key=lambda t: sum(1 for u in near[t] if u not in seen),
        )
        for t in options:
            path.append(t)
            seen.add(t)
            if grow():
                return True
            path.pop()
            seen.discard(t)
        return False

    return list(path) if n > 2 and grow() else list(range(n))


def lookup(index, table):
    n = len(table)
    square = n * n
    total = jnp.int32(0)
    for k, value in enumerate(table):
        if value:
            gap = index - k
            differs = lax.div(gap * gap + (square - 1), jnp.int32(square))
            total = total + value * (1 - differs)
    return total


def ring_kernel(order, per_way, h_ref, out_ref, recv, send, ssem, rsem, free):
    n = len(order)
    where = [0] * n
    for p, s in enumerate(order):
        where[s] = p
    d = lax.axis_index("dp")
    me = lax.axis_index("seq")
    pos = lookup(me, where)
    nxt = lookup(lax.rem(pos + 1, n), order)
    prv = lookup(lax.rem(pos + n - 1, n), order)
    piece = out_ref.shape[0] // per_way
    ahead = (n - 1) // 2
    behind = n - 1 - ahead

    barrier = pltpu.get_barrier_semaphore()
    pl.semaphore_signal(barrier, 1, device_id=(d, nxt), device_id_type=MESH)
    pl.semaphore_signal(barrier, 1, device_id=(d, prv), device_id_type=MESH)
    pl.semaphore_wait(barrier, 2)

    lanes = []
    for forward in (True, False):
        for chunk in range(per_way):
            li = len(lanes)
            lanes.append((recv.at[li], send.at[li], ssem.at[li], rsem.at[li], free.at[li],
                          nxt if forward else prv, prv if forward else nxt,
                          slice(chunk * piece, (chunk + 1) * piece),
                          ahead if forward else behind, forward))
    copies = {}
    for step in range(max(ahead, behind)):
        slot = step % 2
        for li, (recv, send, ssem, rsem, free, to, frm, rows, sends, forward) in enumerate(lanes):
            if step >= sends:
                continue
            if forward:
                target = pos + sends - step
            else:
                target = pos + n - sends + step
            q = lookup(lax.rem(target, n), order)
            own = h_ref[q, rows, :]
            if step == 0:
                part = own
            else:
                copies[(li, step - 1)].wait_recv()
                part = recv[1 - slot].astype(jnp.float32) + own
                if step <= sends - 2:
                    pl.semaphore_signal(free, 1, device_id=(d, frm), device_id_type=MESH)
            if step >= 2:
                copies[(li, step - 2)].wait_send()
                pl.semaphore_wait(free, 1)
            send[slot] = part.astype(send.dtype)
            c = pltpu.make_async_remote_copy(
                src_ref=send.at[slot], dst_ref=recv.at[slot],
                send_sem=ssem.at[slot], recv_sem=rsem.at[slot],
                device_id=(d, to), device_id_type=MESH)
            c.start()
            copies[(li, step)] = c
    for chunk in range(per_way):
        rows = lanes[chunk][7]
        total = h_ref[me, rows, :]
        for li in (chunk, per_way + chunk):
            recv, sends = lanes[li][0], lanes[li][8]
            copies[(li, sends - 1)].wait_recv()
            total = total + recv[(sends - 1) % 2].astype(jnp.float32)
        out_ref[rows, :] = total
    for li, lane in enumerate(lanes):
        sends = lane[8]
        if sends >= 2:
            copies[(li, sends - 2)].wait_send()
        copies[(li, sends - 1)].wait_send()


RING_WAYS = 2


def ring_reduce(h, order, per_way, link_dtype=jnp.bfloat16):
    n, rows, width = h.shape
    lanes = 2 * per_way
    piece = rows // per_way
    return pl.pallas_call(
        functools.partial(ring_kernel, tuple(order), per_way),
        out_shape=jax.ShapeDtypeStruct((rows, width), jnp.float32),
        in_specs=[pl.BlockSpec(memory_space=pltpu.VMEM)],
        out_specs=pl.BlockSpec(memory_space=pltpu.VMEM),
        scratch_shapes=[
            pltpu.VMEM((lanes, 2, piece, width), link_dtype),
            pltpu.VMEM((lanes, 2, piece, width), link_dtype),
            pltpu.SemaphoreType.DMA((lanes, 2)),
            pltpu.SemaphoreType.DMA((lanes, 2)),
            pltpu.SemaphoreType.REGULAR((lanes,)),
        ],
        compiler_params=pltpu.CompilerParams(collective_id=1, has_side_effects=True,
                                             vmem_limit_bytes=48 * 1024 * 1024),
    )(h)


QB = 128


def window_allow(tq_ref, tk_ref, a0, w0):
    rows = lax.broadcasted_iota(jnp.int32, (QB, QB + 2 * HALF), 0)
    cols = lax.broadcasted_iota(jnp.int32, (QB, QB + 2 * HALF), 1)
    offset = cols - rows - HALF
    near = jnp.abs(offset) <= HALF
    same = tk_ref[:, pl.ds(w0, QB + 2 * HALF)] == tq_ref[pl.ds(a0, QB), :]
    return near & (same | (offset == 0))


def nt(a, b):
    return lax.dot_general(a, b, (((1,), (1,)), ((), ())), preferred_element_type=jnp.float32)


def tn(a, b):
    return lax.dot_general(a, b, (((0,), (0,)), ((), ())), preferred_element_type=jnp.float32)


def probs_of(q_ref, kv_ref, allow, a0, w0, h):
    q_h = q_ref[pl.ds(a0, QB), pl.ds(h * HEAD, HEAD)]
    k_h = kv_ref[pl.ds(w0, QB + 2 * HALF), pl.ds(h * HEAD, HEAD)]
    scores = jnp.where(allow, nt(q_h, k_h) * 0.125, -1e30)
    largest = jnp.max(scores, axis=-1, keepdims=True)
    raised = jnp.exp(scores - largest)
    return raised / jnp.sum(raised, axis=-1, keepdims=True), q_h, k_h


def neighbours():
    n_seq = lax.axis_size("seq")
    total = lax.axis_size("dp") * n_seq
    me = lax.axis_index("dp") * n_seq + lax.axis_index("seq")
    before = lax.rem(me + total - 1, total)
    after = lax.rem(me + 1, total)
    return (
        (lax.div(before, n_seq), lax.rem(before, n_seq)),
        (lax.div(after, n_seq), lax.rem(after, n_seq)),
    )


def greet(before, after):
    barrier = pltpu.get_barrier_semaphore()
    pl.semaphore_signal(barrier, 1, device_id=before, device_id_type=MESH)
    pl.semaphore_signal(barrier, 1, device_id=after, device_id_type=MESH)
    pl.semaphore_wait(barrier, 2)


def start_of(b):
    return b * QB if isinstance(b, int) else pl.multiple_of(b * QB, QB)


def attn_fwd_kernel(q_ref, kv_ref, tq_ref, tk_ref, o_ref, lo_ref, hi_ref, wide, send_sem, recv_sem):
    width = q_ref.shape[1]
    count = q_ref.shape[0]
    blocks = count // QB
    before, after = neighbours()
    greet(before, after)
    to_before = pltpu.make_async_remote_copy(
        src_ref=kv_ref.at[pl.ds(0, HALF)], dst_ref=hi_ref,
        send_sem=send_sem.at[0], recv_sem=recv_sem.at[0],
        device_id=before, device_id_type=MESH)
    to_after = pltpu.make_async_remote_copy(
        src_ref=kv_ref.at[pl.ds(count - HALF, HALF)], dst_ref=lo_ref,
        send_sem=send_sem.at[1], recv_sem=recv_sem.at[1],
        device_id=after, device_id_type=MESH)
    to_before.start()
    to_after.start()
    wide[pl.ds(HALF, count), :] = kv_ref[...]

    def block(b, carry):
        a0 = start_of(b)
        allow = window_allow(tq_ref, tk_ref, a0, a0)
        for h in range(HEADS):
            probs, _, _ = probs_of(q_ref, wide, allow, a0, a0, h)
            v_h = wide[pl.ds(a0, QB + 2 * HALF), pl.ds(width + h * HEAD, HEAD)]
            mixed = jnp.dot(probs.astype(jnp.bfloat16), v_h, preferred_element_type=jnp.float32)
            o_ref[pl.ds(a0, QB), pl.ds(h * HEAD, HEAD)] = mixed.astype(o_ref.dtype)
        return carry

    lax.fori_loop(1, blocks - 1, block, 0)
    to_before.wait_recv()
    to_after.wait_recv()
    wide[pl.ds(0, HALF), :] = lo_ref[...]
    wide[pl.ds(count + HALF, HALF), :] = hi_ref[...]
    block(0, 0)
    block(blocks - 1, 0)
    to_before.wait_send()
    to_after.wait_send()


def attn_bwd_kernel(q_ref, kv_ref, lo_ref, hi_ref, tq_ref, tk_ref, do_ref, dq_ref, dkv_ref,
                    wide, dwide, send_lo, send_hi, recv_lo, recv_hi, send_sem, recv_sem):
    width = q_ref.shape[1]
    count = q_ref.shape[0]
    blocks = count // QB
    before, after = neighbours()
    greet(before, after)
    wide[pl.ds(0, HALF), :] = lo_ref[...]
    wide[pl.ds(HALF, count), :] = kv_ref[...]
    wide[pl.ds(count + HALF, HALF), :] = hi_ref[...]
    dwide[...] = jnp.zeros(dwide.shape, dwide.dtype)

    def block(b, carry):
        a0 = start_of(b)
        allow = window_allow(tq_ref, tk_ref, a0, a0)
        for h in range(HEADS):
            probs, q_h, k_h = probs_of(q_ref, wide, allow, a0, a0, h)
            v_h = wide[pl.ds(a0, QB + 2 * HALF), pl.ds(width + h * HEAD, HEAD)]
            do_h = do_ref[pl.ds(a0, QB), pl.ds(h * HEAD, HEAD)]
            grad_probs = nt(do_h, v_h)
            inner = jnp.sum(probs * grad_probs, axis=-1, keepdims=True)
            grad_scores = (probs * (grad_probs - inner)).astype(jnp.bfloat16)
            dq_ref[pl.ds(a0, QB), pl.ds(h * HEAD, HEAD)] = (
                jnp.dot(grad_scores, k_h, preferred_element_type=jnp.float32) * 0.125
            )
            rows = pl.ds(a0, QB + 2 * HALF)
            dwide[rows, pl.ds(h * HEAD, HEAD)] += tn(grad_scores, q_h) * 0.125
            dwide[rows, pl.ds(width + h * HEAD, HEAD)] += tn(probs.astype(jnp.bfloat16), do_h)
        return carry

    block(0, 0)
    block(blocks - 1, 0)
    send_lo[...] = dwide[pl.ds(0, HALF), :].astype(send_lo.dtype)
    send_hi[...] = dwide[pl.ds(count + HALF, HALF), :].astype(send_hi.dtype)
    to_before = pltpu.make_async_remote_copy(
        src_ref=send_lo, dst_ref=recv_hi,
        send_sem=send_sem.at[0], recv_sem=recv_sem.at[0],
        device_id=before, device_id_type=MESH)
    to_after = pltpu.make_async_remote_copy(
        src_ref=send_hi, dst_ref=recv_lo,
        send_sem=send_sem.at[1], recv_sem=recv_sem.at[1],
        device_id=after, device_id_type=MESH)
    to_before.start()
    to_after.start()
    lax.fori_loop(1, blocks - 1, block, 0)
    dkv_ref[...] = dwide[pl.ds(HALF, count), :]
    to_before.wait_recv()
    to_after.wait_recv()
    dkv_ref[pl.ds(0, HALF), :] += recv_lo[...].astype(jnp.float32)
    dkv_ref[pl.ds(count - HALF, HALF), :] += recv_hi[...].astype(jnp.float32)
    to_before.wait_send()
    to_after.wait_send()


VMEM_LIMIT = 48 * 1024 * 1024


def attn_fwd(query, kv, tag_q, tag_k):
    count, width = query.shape
    vm = pl.BlockSpec(memory_space=pltpu.VMEM)
    halo = jax.ShapeDtypeStruct((HALF, kv.shape[1]), kv.dtype)
    return pl.pallas_call(
        attn_fwd_kernel,
        out_shape=(jax.ShapeDtypeStruct((count, width), jnp.bfloat16), halo, halo),
        in_specs=[vm] * 4,
        out_specs=(vm, vm, vm),
        scratch_shapes=[
            pltpu.VMEM((count + 2 * HALF, kv.shape[1]), kv.dtype),
            pltpu.SemaphoreType.DMA((2,)),
            pltpu.SemaphoreType.DMA((2,)),
        ],
        compiler_params=pltpu.CompilerParams(
            collective_id=2, has_side_effects=True, vmem_limit_bytes=VMEM_LIMIT
        ),
    )(query, kv, tag_q.reshape(count, 1), tag_k.reshape(1, -1))


def attn_bwd(query, kv, lo, hi, tag_q, tag_k, grad_out):
    count, width = query.shape
    vm = pl.BlockSpec(memory_space=pltpu.VMEM)
    return pl.pallas_call(
        attn_bwd_kernel,
        out_shape=(
            jax.ShapeDtypeStruct((count, width), jnp.float32),
            jax.ShapeDtypeStruct(kv.shape, jnp.float32),
        ),
        in_specs=[vm] * 7,
        out_specs=(vm, vm),
        scratch_shapes=[
            pltpu.VMEM((count + 2 * HALF, kv.shape[1]), kv.dtype),
            pltpu.VMEM((count + 2 * HALF, kv.shape[1]), jnp.float32),
            pltpu.VMEM((HALF, kv.shape[1]), jnp.bfloat16),
            pltpu.VMEM((HALF, kv.shape[1]), jnp.bfloat16),
            pltpu.VMEM((HALF, kv.shape[1]), jnp.bfloat16),
            pltpu.VMEM((HALF, kv.shape[1]), jnp.bfloat16),
            pltpu.SemaphoreType.DMA((2,)),
            pltpu.SemaphoreType.DMA((2,)),
        ],
        compiler_params=pltpu.CompilerParams(
            collective_id=3, has_side_effects=True, vmem_limit_bytes=VMEM_LIMIT
        ),
    )(query, kv, lo, hi, tag_q.reshape(count, 1), tag_k.reshape(1, -1), grad_out)


ROPE_ROWS = 256


def head_rotate(x):
    width = x.shape[-1]
    lane = lax.broadcasted_iota(jnp.int32, x.shape, x.ndim - 1)
    ahead = pltpu.roll(x, width - HEAD // 2, x.ndim - 1)
    behind = pltpu.roll(x, HEAD // 2, x.ndim - 1)
    return jnp.where(lane % HEAD < HEAD // 2, -ahead, behind)


def rope_fwd_kernel(qkv_ref, cos_ref, sin_ref, q_ref, kv_ref):
    width = q_ref.shape[1]
    c = cos_ref[...]
    s = sin_ref[...]
    q = qkv_ref[:, pl.ds(0, width)]
    k = qkv_ref[:, pl.ds(width, width)]
    q_ref[...] = (q * c + head_rotate(q) * s).astype(q_ref.dtype)
    kv_ref[:, pl.ds(0, width)] = (k * c + head_rotate(k) * s).astype(kv_ref.dtype)
    kv_ref[:, pl.ds(width, width)] = qkv_ref[:, pl.ds(2 * width, width)].astype(kv_ref.dtype)


def rope_bwd_kernel(dq_ref, dkv_ref, cos_ref, sin_ref, out_ref):
    width = dq_ref.shape[1]
    c = cos_ref[...]
    s = sin_ref[...]
    dq = dq_ref[...]
    dk = dkv_ref[:, pl.ds(0, width)]
    out_ref[:, pl.ds(0, width)] = (dq * c - head_rotate(dq) * s).astype(out_ref.dtype)
    out_ref[:, pl.ds(width, width)] = (dk * c - head_rotate(dk) * s).astype(out_ref.dtype)
    out_ref[:, pl.ds(2 * width, width)] = dkv_ref[:, pl.ds(width, width)].astype(out_ref.dtype)


def rows_spec(cols):
    return pl.BlockSpec((ROPE_ROWS, cols), lambda i: (i, 0))


def rope_fwd(qkv, cosine, sine):
    count, width = cosine.shape
    return pl.pallas_call(
        rope_fwd_kernel,
        grid=(count // ROPE_ROWS,),
        out_shape=(
            jax.ShapeDtypeStruct((count, width), jnp.bfloat16),
            jax.ShapeDtypeStruct((count, 2 * width), jnp.bfloat16),
        ),
        in_specs=[rows_spec(3 * width), rows_spec(width), rows_spec(width)],
        out_specs=(rows_spec(width), rows_spec(2 * width)),
    )(qkv, cosine, sine)


def rope_bwd(dq, dkv, cosine, sine):
    count, width = cosine.shape
    return pl.pallas_call(
        rope_bwd_kernel,
        grid=(count // ROPE_ROWS,),
        out_shape=jax.ShapeDtypeStruct((count, 3 * width), jnp.bfloat16),
        in_specs=[rows_spec(width), rows_spec(2 * width), rows_spec(width), rows_spec(width)],
        out_specs=rows_spec(3 * width),
    )(dq, dkv, cosine, sine)


def gain_rows(gain, width, rows=8):
    line = jnp.pad(gain, (0, width - gain.shape[0]))
    return jnp.concatenate([line[None], jnp.zeros((rows - 1, width), gain.dtype)], 0)


def gather_rows(payload, n_dp, n_seq):
    every = lax.all_gather(payload, ("dp", "seq"), axis=0, tiled=True)
    return every.reshape(n_dp, n_seq, payload.shape[0], payload.shape[1])


def gain_blocks(grad_gain, n_dp, n_seq, width, height=8):
    part = jnp.pad(grad_gain.reshape(n_seq, -1), ((0, 0), (0, width - grad_gain.shape[0] // n_seq)))
    rows = jnp.concatenate([part[:, None], jnp.zeros((n_seq, height - 1, width), part.dtype)], 1)
    return jnp.broadcast_to(rows[None], (n_dp, n_seq, height, width))


def front(value, n_dp):
    return value.reshape(value.shape[0], n_dp, -1)


def apply_t(left, weight_t, n_dp):
    return jnp.einsum("tdr,dnr->tn", front(left, n_dp), weight_t, preferred_element_type=jnp.float32)


def apply_back(grad, weight_t):
    out = jnp.einsum("tn,dnr->tdr", grad, weight_t, preferred_element_type=jnp.float32)
    return out.reshape(out.shape[0], -1)


def grad_t(grad, left, n_dp):
    width = left.shape[1] // n_dp
    return [
        lax.dot_general(
            grad,
            left[:, d * width : (d + 1) * width],
            (((0,), (0,)), ((), ())),
            preferred_element_type=jnp.float32,
        )
        for d in range(n_dp)
    ]


def on_device(order, tokens, doc_start, real, w_qkv, w_out, w_in, w_down, gain_attn, gain_mlp, cotangent):
    count = tokens.shape[0]
    n_dp, n_seq = lax.axis_size("dp"), lax.axis_size("seq")
    rows, qkv_cols = w_qkv.shape
    out_cols, in_cols = w_out.shape[1], w_in.shape[1]
    down_rows, down_cols = w_down.shape
    down_lines = down_rows * down_cols // rows
    first = gather_rows(jnp.concatenate([w_qkv.T, gain_rows(gain_attn, rows)], 0), n_dp, n_seq)
    second = gather_rows(
        jnp.concatenate(
            [w_out.T, w_in.T, w_down.T.reshape(down_lines, rows), gain_rows(gain_mlp, rows)], 0
        ),
        n_dp,
        n_seq,
    )
    full_qkv = first[:, :, :qkv_cols].reshape(n_dp, n_seq * qkv_cols, rows)
    gain_one = first[0, :, qkv_cols, : gain_attn.shape[0]].reshape(-1).astype(jnp.float32)
    stream = tokens.astype(jnp.float32)
    normed_a, factor_a = layer_norm(stream)
    h_attn = (normed_a * gain_one).astype(jnp.bfloat16)
    qkv = apply_t(h_attn, full_qkv, n_dp)
    offset_base = lax.axis_index(("dp", "seq")) * count
    place = (offset_base + jnp.arange(count, dtype=jnp.int32) - doc_start).astype(jnp.float32)
    cosine, sine = rotary_tables(place)
    query, key_value = rope_fwd(qkv, cosine, sine)
    tag_query = doc_start + 1
    tag_key = jnp.where(real == 1, tag_query, 0)
    wide_tag = padded(tag_key, ((("dp", "seq"), 0),), HALF)
    attn_out, halo_lo, halo_hi = attn_fwd(query, key_value, tag_query, wide_tag)
    attn_out, second = lax.optimization_barrier((attn_out, second))
    at = 0
    full_out = second[:, :, at : at + out_cols].reshape(n_dp, n_seq * out_cols, rows)
    at += out_cols
    full_in = second[:, :, at : at + in_cols].reshape(n_dp, n_seq * in_cols, rows)
    at += in_cols
    full_down = (
        second[:, :, at : at + down_lines]
        .reshape(n_dp, n_seq, down_cols, down_rows)
        .reshape(n_dp, n_seq * down_cols, down_rows)
    )
    at += down_lines
    gain_two = second[0, :, at, : gain_mlp.shape[0]].reshape(-1).astype(jnp.float32)
    mid = stream + apply_t(attn_out, full_out, n_dp)
    normed_m, factor_m = layer_norm(mid)
    h_mlp = (normed_m * gain_two).astype(jnp.bfloat16)
    gate_up = apply_t(h_mlp, full_in, n_dp)
    hidden_out, glu_pull = jax.vjp(glu_piece, gate_up)
    hidden = hidden_out.astype(jnp.bfloat16)
    result = mid + apply_t(hidden, full_down, n_dp)
    output = result.astype(jnp.bfloat16)
    grad_down = grad_t(cotangent, hidden, n_dp)
    grad_hidden = apply_back(cotangent, full_down)
    grad_gate_up = glu_pull(grad_hidden)[0].astype(jnp.bfloat16)
    grad_inw = grad_t(grad_gate_up, h_mlp, n_dp)
    grad_hmlp = apply_back(grad_gate_up, full_in)
    grad_gain_two = jnp.sum(grad_hmlp * normed_m, axis=0)
    grad_mid = cotangent.astype(jnp.float32) + norm_back(grad_hmlp * gain_two, normed_m, factor_m)
    grad_branch = grad_mid.astype(jnp.bfloat16)
    grad_outw = grad_t(grad_branch, attn_out, n_dp)
    grad_attn = apply_back(grad_branch, full_out).astype(jnp.bfloat16)
    grad_query, grad_kv = attn_bwd(query, key_value, halo_lo, halo_hi, tag_query, wide_tag, grad_attn)
    grad_qkv = rope_bwd(grad_query, grad_kv, cosine, sine)
    grad_qkvw = grad_t(grad_qkv, h_attn, n_dp)
    grad_hattn = apply_back(grad_qkv, full_qkv)
    grad_gain_one = jnp.sum(grad_hattn * normed_a, axis=0)
    grad_tokens = grad_mid + norm_back(grad_hattn * gain_one, normed_a, factor_a)
    height = out_cols + in_cols + down_lines + qkv_cols + 8
    tail = 8 + (-height) % (RING_WAYS * 16)
    gain_both = jnp.concatenate(
        [
            gain_blocks(grad_gain_two, 1, n_seq, rows, 1)[0],
            gain_blocks(grad_gain_one, 1, n_seq, rows, tail - 1)[0],
        ],
        1,
    )
    blocks = jnp.stack(
        [
            jnp.concatenate(
                [
                    *lax.optimization_barrier(
                        (
                            grad_outw[d].reshape(n_seq, out_cols, rows),
                            grad_inw[d].reshape(n_seq, in_cols, rows),
                            grad_down[d]
                            .reshape(n_seq, down_cols, down_rows)
                            .reshape(n_seq, down_lines, rows),
                            grad_qkvw[d].reshape(n_seq, qkv_cols, rows),
                            gain_both,
                        )
                    ),
                ],
                1,
            )
            for d in range(n_dp)
        ]
    )
    depth = blocks.shape[2]
    half = lax.psum_scatter(
        blocks.reshape(n_dp, n_seq * depth, rows), "dp", scatter_dimension=0, tiled=True
    )
    late = ring_reduce(half.reshape(n_seq, depth, rows), order, RING_WAYS)
    at = 0
    late_out = late[at : at + out_cols].T
    at += out_cols
    late_in = late[at : at + in_cols].T
    at += in_cols
    late_down = late[at : at + down_lines].reshape(down_cols, down_rows).T
    at += down_lines
    late_qkv = late[at : at + qkv_cols].T
    at += qkv_cols
    late_gain_two = late[at, : gain_mlp.shape[0]]
    late_gain_one = late[at + 1, : gain_attn.shape[0]]
    return (
        output,
        grad_tokens,
        late_qkv,
        late_out,
        late_in,
        late_down,
        late_gain_one,
        late_gain_two,
    )


def solution(mesh):
    placed = (
        P(("dp", "seq"), None),
        P(("dp", "seq")),
        P(("dp", "seq")),
        P("dp", "seq"),
        P("dp", "seq"),
        P("dp", "seq"),
        P("dp", "seq"),
        P("seq"),
        P("seq"),
        P(("dp", "seq"), None),
    )
    return jax.shard_map(
        functools.partial(on_device, ring_order(mesh)),
        mesh=mesh,
        in_specs=placed,
        out_specs=(
            P(("dp", "seq"), None),
            P(("dp", "seq"), None),
            P("dp", "seq"),
            P("dp", "seq"),
            P("dp", "seq"),
            P("dp", "seq"),
            P("seq"),
            P("seq"),
        ),
        check_vma=False,
    )
```

profile of v0, /device:TPU:0, one launch (start us, length us, event | category | flops | bytes accessed | tf_op | source)
XLA Modules:
  0.0 466.8 jit_solution(8453891042323907756)
XLA Ops:
  7.9 1.6 pad_maximum_fusion.3
  11.2 4.2 concatenate.29
  16.2 4.8 %collective-permute-start = (s32[64]{0:T(128)S(1)}, s32[64]{0:T(128)S(1)}, u32[]{:S(2)}, u32[]{:S(2)}) collective-permute-start(s32[64]{0:T(128)S(1)} %get-tuple-element.79), channel_id=1, source_target_pairs={{0,1},{1,2},{2,3},{3,4},{4,5},{5,6},{6,7},{7,8},{8,9},{9,10},{10,1... | collective-permute-start | bytes 776 | tf_op jit(solution)/shard_map/ppermute | solution.py:25
  21.0 1.3 collective-permute-start.1
  22.3 1.7 copy.28
  24.7 2.1 tile.8
  26.7 3.6 copy.30.cos_ref
  30.3 2.1 tile.20
  32.4 3.6 copy.31.sin_ref
  36.9 2.6 copy.38
  39.7 35.1 %all-gather.3.cloned.1.call-done = bf16[4864,384]{1,0:T(8,128)(2,1)} async-done(((bf16[152,384]{1,0:T(8,128)(2,1)}), bf16[4864,384]{1,0:T(8,128)(2,1)}) %all-gather.3.cloned.1.call-update) | async-done | bytes 3735568 | tf_op jit(solution)/shard_map/all_gather | solution.py:490
  74.8 4.2 slice.97
  79.8 5.8 %copy.47 = bf16[2,384,2304]{2,1,0:T(8,128)(2,1)} copy(bf16[2,384,2304]{1,2,0:T(8,128)(2,1)} %bitcast.93) | data formatting | bytes 7077888 | tf_op jit(solution)/shard_map/tn,dnr->tdr/dot_general | solution.py:509
  86.2 1.1 copy-done.26
  87.3 8.3 %convolution_bitcast_fusion.1.qkv_ref = f32[1024,2304]{1,0:T(8,128)} fusion(bf16[1024,2,384]{0,2,1:T(8,128)(2,1)S(1)} %bitcast.120, bf16[2,2304,384]{2,1,0:T(8,128)(2,1)} %bitcast.94), kind=kOutput, calls=%fused_computation.4 | convolution fusion | flops 3623878656 | bytes 14548992 | tf_op jit(solution)/shard_map/tdr,dnr->tn/dot_general | solution.py:505
  95.6 9.3 %shard_map.161 = (bf16[1024,768]{1,0:T(8,128)(2,1)}, bf16[1024,1536]{1,0:T(8,128)(2,1)}) custom-call(f32[1024,2304]{1,0:T(8,128)} %convolution_bitcast_fusion.1.qkv_ref, f32[1024,768]{1,0:T(8,128)} %copy.30.cos_ref, f32[1024,768]{1,0:T(8,128)} %copy.31.sin_ref), custom_call_target="tpu_custom_call" | custom-call | tf_op jit(solution)/shard_map/pallas_call | solution.py:461
  104.9 1.4 copy-done
  106.3 24.9 %shard_map.162 = (bf16[1024,768]{1,0:T(8,128)(2,1)S(1)}, bf16[64,1536]{1,0:T(8,128)(2,1)S(1)}, bf16[64,1536]{1,0:T(8,128)(2,1)S(1)}) custom-call(bf16[1024,768]{1,0:T(8,128)(2,1)S(1)} %copy-done, bf16[1024,1536]{1,0:T(8,128)(2,1)} %get-tuple-element.28.kv_ref, s32[1024,1]{1,0:T(8,128)S(1)} %copy.32.tq_ref, s32[1,1152]{1,0:T(1,128)S(1)} %reshape.170.tk_ref), custom_call_target="tpu_custom_call" | custom-call | tf_op jit(solution)/shard_map/pallas_call | solution.py:379
  131.2 19.2 %all-gather.5.cloned.1.call-done = bf16[8704,384]{1,0:T(8,128)(2,1)} async-done(((bf16[272,384]{1,0:T(8,128)(2,1)}), bf16[8704,384]{1,0:T(8,128)(2,1)}) %all-gather.5.cloned.1.call-update) | async-done | bytes 6684688 | tf_op jit(solution)/shard_map/all_gather | solution.py:490
  150.4 2.4 slice.76
  152.8 2.9 slice.81
  156.5 4.2 slice.78
  160.7 4.8 %reshape_reshape.9 = bf16[2,768,576]{2,1,0:T(8,128)(2,1)} reshape(bf16[2,16,72,384]{3,2,1,0:T(8,128)(2,1)} %slice.81) | data formatting | bytes 3538944 | tf_op jit(solution)/shard_map/reshape;reshape | solution.py:564
  165.5 6.6 %fusion.23 = f32[2,576,1024]{2,1,0:T(8,128)} fusion(bf16[2,768,576]{2,1,0:T(8,128)(2,1)} %reshape_reshape.9, bf16[1024,768]{1,0:T(8,128)(2,1)} %param.19), kind=kOutput, calls=%fused_computation.52 | convolution fusion | flops 1811939328 | bytes 8060928 | tf_op jit(solution)/shard_map/tn,dnr->tdr/dot_general | solution.py:509
  172.0 6.3 %copy.40 = f32[1024,1152]{1,0:T(8,128)} copy(f32[1024,1152]{0,1:T(8,128)} %bitcast.106) | data formatting | bytes 9437184 | tf_op jit(solution)/shard_map/reshape | solution.py:510
  178.4 3.2 fusion.47
  183.2 1.2 copy-done.28
  185.3 3.9 convolution_bitcast_fusion
  189.2 11.1 %fusion.25 = (f32[1024,1152]{1,0:T(8,128)}, f32[1024,1152]{1,0:T(8,128)S(1)}) fusion(f32[1024,1152]{1,0:T(8,128)S(1)} %bitcast.90, f32[1024,2304]{1,0:T(8,128)S(1)} %convolution_bitcast_fusion), kind=kLoop, calls=%fused_computation.56 | loop fusion | flops 76677120 | bytes 18874368 | tf_op jit(solution)/shard_map/transpose(jvp())/mul | solution.py:80
  200.4 4.3 multiply_add_fusion
  204.7 5.8 %copy.42 = bf16[2,384,2304]{2,1,0:T(8,128)(2,1)} copy(bf16[2,384,2304]{1,2,0:T(8,128)(2,1)} %bitcast.91) | data formatting | bytes 7077888 | tf_op jit(solution)/shard_map/tn,dnr->tdr/dot_general | solution.py:509
  210.5 8.5 %fusion.30 = f32[2304,384]{1,0:T(8,128)} fusion(bf16[1024,768]{0,1:T(8,128)(2,1)} %copy-done.28, f32[1024,1152]{1,0:T(8,128)} %get-tuple-element.70, f32[1024,1152]{1,0:T(8,128)} %get-tuple-element.68), kind=kOutput, calls=%fused_computation.61 | convolution fusion | flops 1816657920 | bytes 13762560 | tf_op jit(solution)/shard_map/dot_general | solution.py:516
  219.0 7.0 %multiply_reduce_fusion = (f32[768]{0:T(1024)S(1)}, f32[1024]{0:T(1024)S(1)}, f32[1024]{0:T(1024)S(1)}, f32[1024,768]{0,1:T(8,128)S(1)}) fusion(f32[1024,768]{0,1:T(8,128)S(1)} %copy-done.7, f32[1024]{0:T(1024)S(1)} %add_rsqrt_fusion, f32[1024]{0:T(1024)S(1)} %broadcast_multiply_fusion.4, f32[768]{0:T(1024)S(1)} %reshape.190, ...), kind=kOutput, calls=%fused_computation.41 | convolution fusion | flops 3634885888 | bytes 19290112 | tf_op jit(solution)/shard_map/tn,dnr->tdr/dot_general | solution.py:509
  227.0 2.1 fusion.36
  229.1 2.0 fusion.38
  231.1 4.5 fusion.34
  235.7 2.7 convolution_bitcast_fusion.2
  238.3 2.4 convolution_bitcast_fusion.3
  241.5 3.5 convolution_convert_fusion.do_ref
  245.1 58.2 %shard_map.163 = (f32[1024,768]{1,0:T(8,128)}, f32[1024,1536]{1,0:T(8,128)}) custom-call(bf16[1024,768]{1,0:T(8,128)(2,1)S(1)} %copy-done.1, bf16[1024,1536]{1,0:T(8,128)(2,1)} %get-tuple-element.28.kv_ref, bf16[64,1536]{1,0:T(8,128)(2,1)S(1)} %get-tuple-element.32.lo_ref, bf16[64,1536]{1,0:T(8,128)(2,1)S(1)} %get-tuple-element.33.hi_ref, ...), custom_call_target="tpu_custom_call" | custom-call | tf_op jit(solution)/shard_map/pallas_call | solution.py:398
  303.3 9.8 %shard_map.164 = bf16[1024,2304]{1,0:T(8,128)(2,1)} custom-call(f32[1024,768]{1,0:T(8,128)} %get-tuple-element.34.dq_ref, f32[1024,1536]{1,0:T(8,128)} %get-tuple-element.35.dkv_ref, f32[1024,768]{1,0:T(8,128)} %copy.30.cos_ref, f32[1024,768]{1,0:T(8,128)} %copy.31.sin_ref), custom_call_target="tpu_custom_call" | custom-call | tf_op jit(solution)/shard_map/pallas_call | solution.py:475
  313.1 7.0 %fusion.28 = f32[2304,384]{1,0:T(8,128)} fusion(bf16[1024,2304]{1,0:T(8,128)(2,1)} %shard_map.164, bf16[1024,768]{0,1:T(8,128)(2,1)S(1)} %copy-done.27), kind=kOutput, calls=%fused_computation.59 | convolution fusion | flops 1811939328 | bytes 9043968 | tf_op jit(solution)/shard_map/dot_general | solution.py:516
  320.1 4.5 fusion.32
  324.6 5.8 %fusion.18 = (f32[768]{0:T(1024)S(1)}, f32[1024]{0:T(1024)S(1)}, f32[1024]{0:T(1024)S(1)}, f32[1024,768]{0,1:T(8,128)}) fusion(bf16[1024,768]{0,1:T(8,128)(2,1)S(1)} %copy-done.5, f32[1024]{0:T(1024)S(1)} %add_rsqrt_fusion.1, f32[1024]{0:T(1024)S(1)} %broadcast_multiply_fusion.5, f32[768]{0:T(1024)S(1)} %reshape.189, bf16[1024,2304]{1,0:T(8,128)(2,1)S(1)} %copy-done.16, ...), kind=kOutput, calls=%fused_computation.37 | convolution fusion | flops 3630953728 | bytes 12998656 | tf_op jit(solution)/shard_map/tn,dnr->tdr/dot_general | solution.py:509
  330.4 1.9 copy.49
  332.4 2.5 reshape_reshape.11
  335.2 1.2 constant_dynamic-update-slice_fusion.9
  336.3 2.2 copy.48
  338.6 2.4 reshape_reshape.10
  341.1 4.2 constant_dynamic-update-slice_fusion.8
  345.4 1.4 constant_dynamic-update-slice_fusion.7
  346.7 1.3 copy-done.23
  348.0 2.1 constant_dynamic-update-slice_fusion.6
  351.7 1.1 copy-done.13
  354.3 2.8 copy-done.10
  357.1 7.2 %pad_maximum_fusion = f32[2,6656,384]{2,1,0:T(8,128)} fusion(f32[1,6656,384]{2,1,0:T(8,128)S(1)} %bitcast.96, f32[1,6656,384]{2,1,0:T(8,128)S(1)} %bitcast.95), kind=kLoop, calls=%fused_computation | loop fusion | flops 5111808 | bytes 40894464 | tf_op jit(solution)/shard_map/stack | solution.py:601
  364.3 4.4 copy.35
  368.7 5.8 %fusion.20 = bf16[1024,768]{0,1:T(8,128)(2,1)} fusion(f32[1024,768]{0,1:T(8,128)S(1)} %copy-done.8, bf16[2,768,576]{2,1,0:T(8,128)(2,1)} %reshape_reshape.9, bf16[1024,2,576]{0,2,1:T(8,128)(2,1)} %bitcast.119), kind=kOutput, calls=%fused_computation.40 | convolution fusion | flops 1813512192 | bytes 8847360 | tf_op jit(solution)/shard_map/tdr,dnr->tn/dot_general | solution.py:505
  374.5 3.0 copy.50
  377.6 1.0 copy-done.3
  378.6 6.4 %fusion.17 = f32[1024,768]{0,1:T(8,128)} fusion(f32[1024,768]{0,1:T(8,128)S(1)} %copy-done.3, bf16[1024,768]{0,1:T(8,128)(2,1)} %copy-done.4, f32[1024,768]{0,1:T(8,128)} %get-tuple-element.86, f32[1024]{0:T(1024)S(1)} %broadcast_multiply_fusion, f32[1024]{0:T(1024)S(1)} %broadcast_multiply_fusion.1, f32[768]{0:T(1024)S(1)} %reshape.189, ...), kind=kLoop, calls=%fused_computation.36 | loop fusion | flops 7077888 | bytes 11029504 | tf_op jit(solution)/shard_map/add | solution.py:591
  384.9 4.3 copy.51
  389.3 3.8 reduce-scatter.2.cloned.1.call-done
  393.1 64.0 %shard_map.165 = f32[416,384]{1,0:T(8,128)S(1)} custom-call(f32[16,416,384]{2,1,0:T(8,128)} %bitcast.99), custom_call_target="tpu_custom_call" | custom-call | tf_op jit(solution)/shard_map/pallas_call | solution.py:210
  (124 shorter events, 17.8 us)
Async XLA Ops:
  7.2 67.7 %all-gather.3.cloned.1.call-start = ((), (), s32[]{:S(2)}) async-start(), calls=%async_computation.1 | async-start | bytes 3852288 | tf_op jit(solution)/shard_map/all_gather | solution.py:490
  9.5 141.0 %all-gather.5.cloned.1.call-start = ((), (), s32[]{:S(2)}) async-start(), calls=%async_computation.2 | async-start | bytes 6893568 | tf_op jit(solution)/shard_map/all_gather | solution.py:490
  15.4 377.8 %reduce-scatter.2.cloned.1.call-start = ((), (), s32[]{:S(2)}) async-start(), calls=%async_computation.3 | async-start | bytes 30670848 | tf_op jit(solution)/shard_map/reduce_scatter | solution.py:623
  16.2 23.4 %collective-permute-start = (s32[64]{0:T(128)S(1)}, s32[64]{0:T(128)S(1)}, u32[]{:S(2)}, u32[]{:S(2)}) collective-permute-start(s32[64]{0:T(128)S(1)} %get-tuple-element.79), channel_id=1, source_target_pairs={{0,1},{1,2},{2,3},{3,4},{4,5},{5,6},{6,7},{7,8},{8,9},{9,10},{10,1... | collective-permute-start | bytes 776 | tf_op jit(solution)/shard_map/ppermute | solution.py:25
  21.0 18.6 %collective-permute-start.1 = (s32[64]{0:T(128)S(1)}, s32[64]{0:T(128)S(1)}, u32[]{:S(2)}, u32[]{:S(2)}) collective-permute-start(s32[64]{0:T(128)S(1)} %get-tuple-element.78), channel_id=1, source_target_pairs={{1,0},{2,1},{3,2},{4,3},{5,4},{6,5},{7,6},{8,7},{9,8},{10,9},{11,1... | collective-permute-start | bytes 776 | tf_op jit(solution)/shard_map/ppermute | solution.py:26
  24.1 61.6 %copy-start.4 = (bf16[1024,768]{0,1:T(8,128)(2,1)}, bf16[1024,768]{0,1:T(8,128)(2,1)S(1)}, u32[]{:S(2)}) copy-start(bf16[1024,768]{0,1:T(8,128)(2,1)S(1)} %copy.28) | copy-start | bytes 4718596
  86.1 1.1 copy-start.26
  104.9 1.4 copy-start
  181.6 1.6 copy-start.6
  181.6 3.7 copy-start.9
  182.0 7.2 %slice-start = ((s8[4718592]{0:T(1024)(128)(4,1)}), s8[4194304]{0:T(1024)(128)(4,1)S(1)}, s32[]{:S(2)}) async-start(s8[4718592]{0:T(1024)(128)(4,1)} %bitcast.89), calls=%async_computation.4 | async-start | bytes 8388608
  183.2 1.2 copy-start.28
  185.3 3.9 slice-start.1
  210.5 8.5 %copy-start.7 = (f32[1024,768]{0,1:T(8,128)S(1)}, f32[1024,768]{0,1:T(8,128)}, u32[]{:S(2)}) copy-start(f32[1024,768]{0,1:T(8,128)} %copy-done.6) | copy-start | bytes 9437188
  210.5 8.5 %copy-start.15 = (f32[1024,1152]{1,0:T(8,128)S(1)}, f32[1024,1152]{1,0:T(8,128)}, u32[]{:S(2)}) copy-start(f32[1024,1152]{1,0:T(8,128)} %get-tuple-element.70) | copy-start | bytes 14155780
  210.5 8.5 %copy-start.24 = (bf16[2,384,2304]{2,1,0:T(8,128)(2,1)S(1)}, bf16[2,384,2304]{2,1,0:T(8,128)(2,1)}, u32[]{:S(2)}) copy-start(bf16[2,384,2304]{2,1,0:T(8,128)(2,1)} %copy.42) | copy-start | bytes 10616836
  210.5 20.6 %slice-start.2 = ((s8[4718592]{0:T(1024)(128)(4,1)}), s8[4194304]{0:T(1024)(128)(4,1)S(1)}, s32[]{:S(2)}) async-start(s8[4718592]{0:T(1024)(128)(4,1)} %bitcast.109), calls=%async_computation.6 | async-start | bytes 8388608
  219.0 7.0 %copy-start.14 = (bf16[1024,768]{0,1:T(8,128)(2,1)S(1)}, bf16[1024,768]{0,1:T(8,128)(2,1)}, u32[]{:S(2)}) copy-start(bf16[1024,768]{0,1:T(8,128)(2,1)} %copy.38) | copy-start | bytes 4718596
  219.0 12.1 %slice-start.3 = ((s8[4718592]{0:T(1024)(128)(4,1)}), s8[524288]{0:T(1024)(128)(4,1)S(1)}, s32[]{:S(2)}) async-start(s8[4718592]{0:T(1024)(128)(4,1)} %bitcast.109), calls=%async_computation.7 | async-start | bytes 1048576
  227.0 2.1 copy-start.2
  229.1 2.0 copy-start.29
  231.1 4.5 copy-start.11
  231.1 4.5 copy-start.25
  238.3 2.4 copy-start.19
  241.5 3.5 copy-start.1
  303.2 9.8 %copy-start.27 = (bf16[1024,768]{0,1:T(8,128)(2,1)S(1)}, bf16[1024,768]{0,1:T(8,128)(2,1)}, u32[]{:S(2)}) copy-start(bf16[1024,768]{0,1:T(8,128)(2,1)} %copy-done.26) | copy-start | bytes 4718596
  313.1 7.0 %copy-start.16 = (bf16[1024,2304]{1,0:T(8,128)(2,1)S(1)}, bf16[1024,2304]{1,0:T(8,128)(2,1)}, u32[]{:S(2)}) copy-start(bf16[1024,2304]{1,0:T(8,128)(2,1)} %shard_map.164) | copy-start | bytes 14155780
  320.1 4.5 copy-start.5
  320.1 4.5 copy-start.20
  330.4 4.7 %copy-start.18 = (f32[768,384]{1,0:T(8,128)S(1)}, f32[768,384]{1,0:T(8,128)}, u32[]{:S(2)}) copy-start(f32[768,384]{1,0:T(8,128)} %fusion.36) | copy-start | bytes 3538948
  336.3 4.6 copy-start.17
  341.1 4.3 copy-start.12
  345.4 2.6 copy-start.23
  348.0 3.3 copy-start.21
  351.3 1.5 copy-start.13
  351.3 2.5 copy-start.22
  352.8 4.3 copy-start.10
  364.3 4.4 copy-start.8
  374.5 4.0 copy-start.3
Sparse Core Ops, SparseCore 0:
  11.4 63.3 all-gather.2
  78.3 72.0 all-gather.4
  364.4 28.6 reduce-scatter.1
where the time goes:
time: 476 us; the launch traced here: 467 us
  Pallas kernels  166 us (35%)
  local copies, waits for them, and re-layouts  107 us (22%)
  matrix products  77.8 us (16%)
  waiting for transfers between devices  58.2 us (12%)
  other arithmetic  36.5 us (8%)
  between operations  14.7 us (3%)
  starting transfers between devices  6.24 us (1%)
    pallas_call x1, Pallas kernels, ring_reduce(): pl.pallas_call(functools.partial(ring_kernel, tuple(order), per_way), out...  64 us
    pallas_call x1, Pallas kernels, attn_bwd(): pl.pallas_call(attn_bwd_kernel, out_shape=(jax.ShapeDtypeStruct((count, w...  58.2 us
    all_gather x2, waiting for transfers between devices, gather_rows(): every = lax.all_gather(payload, ('dp', 'seq'), axis=0, tiled=True)  54.3 us
    unnamed x80, local copies, waits for them, and re-layouts  34.6 us
    dot_general x8, matrix products, grad_t(): lax.dot_general(grad, left[:, d * width:(d + 1) * width], (((0,), (0,)),...  33.7 us
    pallas_call x1, Pallas kernels, attn_fwd(): pl.pallas_call(attn_fwd_kernel, out_shape=(jax.ShapeDtypeStruct((count, w...  24.9 us
    dot_general x4, matrix products, apply_back(): jnp.einsum('tn,dnr->tdr', grad, weight_t, preferred_element_type=jnp.floa...  22.8 us
    dot_general x4, matrix products, apply_t(): jnp.einsum('tdr,dnr->tn', front(left, n_dp), weight_t, preferred_element_...  21.3 us
  transfers between devices with their start and end apart: 5, of which 3 were waited for; matrix products, arithmetic and copies ran while one was open for 14% of the time, Pallas kernels for 7%

commit v1 on v0

--- a/solution.py
+++ b/solution.py
@@ -530,16 +530,19 @@
     out_cols, in_cols = w_out.shape[1], w_in.shape[1]
     down_rows, down_cols = w_down.shape
     down_lines = down_rows * down_cols // rows
-    first = gather_rows(jnp.concatenate([w_qkv.T, gain_rows(gain_attn, rows)], 0), n_dp, n_seq)
+    first = gather_rows(
+        jnp.concatenate([w_qkv.T, w_out.T, gain_rows(gain_attn, rows)], 0), n_dp, n_seq
+    )
     second = gather_rows(
-        jnp.concatenate(
-            [w_out.T, w_in.T, w_down.T.reshape(down_lines, rows), gain_rows(gain_mlp, rows)], 0
-        ),
+        jnp.concatenate([w_in.T, w_down.T.reshape(down_lines, rows), gain_rows(gain_mlp, rows)], 0),
         n_dp,
         n_seq,
     )
     full_qkv = first[:, :, :qkv_cols].reshape(n_dp, n_seq * qkv_cols, rows)
-    gain_one = first[0, :, qkv_cols, : gain_attn.shape[0]].reshape(-1).astype(jnp.float32)
+    full_out = first[:, :, qkv_cols : qkv_cols + out_cols].reshape(n_dp, n_seq * out_cols, rows)
+    gain_one = (
+        first[0, :, qkv_cols + out_cols, : gain_attn.shape[0]].reshape(-1).astype(jnp.float32)
+    )
     stream = tokens.astype(jnp.float32)
     normed_a, factor_a = layer_norm(stream)
     h_attn = (normed_a * gain_one).astype(jnp.bfloat16)
@@ -552,10 +555,9 @@
     tag_key = jnp.where(real == 1, tag_query, 0)
     wide_tag = padded(tag_key, ((("dp", "seq"), 0),), HALF)
     attn_out, halo_lo, halo_hi = attn_fwd(query, key_value, tag_query, wide_tag)
-    attn_out, second = lax.optimization_barrier((attn_out, second))
+    mid = stream + apply_t(attn_out, full_out, n_dp)
+    mid, second = lax.optimization_barrier((mid, second))
     at = 0
-    full_out = second[:, :, at : at + out_cols].reshape(n_dp, n_seq * out_cols, rows)
-    at += out_cols
     full_in = second[:, :, at : at + in_cols].reshape(n_dp, n_seq * in_cols, rows)
     at += in_cols
     full_down = (
@@ -565,7 +567,6 @@
     )
     at += down_lines
     gain_two = second[0, :, at, : gain_mlp.shape[0]].reshape(-1).astype(jnp.float32)
-    mid = stream + apply_t(attn_out, full_out, n_dp)
     normed_m, factor_m = layer_norm(mid)
     h_mlp = (normed_m * gain_two).astype(jnp.bfloat16)
     gate_up = apply_t(h_mlp, full_in, n_dp)

time: 476 us -> 467 us (0.981)
  local copies, waits for them, and re-layouts: 107 us -> 85.5 us
  other arithmetic: 36.5 us -> 43.2 us
  waiting for transfers between devices: 58.2 us -> 64.4 us
    unnamed x80 -> x78, local copies, waits for them, and re-layouts: 34.6 us -> 17 us
    reduce_scatter x1, waiting for transfers between devices: 3.85 us -> 13.3 us  [on_device(): lax.psum_scatter(blocks.reshape(n_dp, n_seq * depth, rows), 'dp', scatter...]
  transfers between devices with their start and end apart: 5 -> 5, of which waited for: 3 -> 3; matrix products, arithmetic and copies ran while one was open for 14% -> 12% of each run, Pallas kernels for 7% -> 7%
where the time goes in v1:
time: 467 us; the launch traced here: 459 us
  Pallas kernels  166 us (36%)
  local copies, waits for them, and re-layouts  85.5 us (18%)
  matrix products  77.4 us (17%)
  waiting for transfers between devices  64.4 us (14%)
  other arithmetic  43.2 us (9%)
  between operations  14.8 us (3%)
  starting transfers between devices  6.87 us (1%)
    pallas_call x1, Pallas kernels, ring_reduce(): pl.pallas_call(functools.partial(ring_kernel, tuple(order), per_way), out...  64 us
    pallas_call x1, Pallas kernels, attn_bwd(): pl.pallas_call(attn_bwd_kernel, out_shape=(jax.ShapeDtypeStruct((count, w...  58.2 us
    all_gather x2, waiting for transfers between devices, gather_rows(): every = lax.all_gather(payload, ('dp', 'seq'), axis=0, tiled=True)  51 us
    dot_general x8, matrix products, grad_t(): lax.dot_general(grad, left[:, d * width:(d + 1) * width], (((0,), (0,)),...  29.7 us
    dot_general x4, matrix products, apply_back(): jnp.einsum('tn,dnr->tdr', grad, weight_t, preferred_element_type=jnp.floa...  26.4 us
    pallas_call x1, Pallas kernels, attn_fwd(): pl.pallas_call(attn_fwd_kernel, out_shape=(jax.ShapeDtypeStruct((count, w...  25 us
    dot_general x4, matrix products, apply_t(): jnp.einsum('tdr,dnr->tn', front(left, n_dp), weight_t, preferred_element_...  21.4 us
    unnamed x78, local copies, waits for them, and re-layouts  17 us
  transfers between devices with their start and end apart: 5, of which 3 were waited for; matrix products, arithmetic and copies ran while one was open for 12% of the time, Pallas kernels for 7%

profile of v1, /device:TPU:0, one launch (start us, length us, event | category | flops | bytes accessed | tf_op | source)
XLA Modules:
  0.0 458.6 jit_solution(14314296903028620556)
XLA Ops:
  7.9 1.6 pad_maximum_fusion.4
  11.2 1.6 pad_maximum_fusion.3
  13.7 1.3 collective-permute-start.1
  14.9 5.5 %collective-permute-start = (s32[64]{0:T(128)S(1)}, s32[64]{0:T(128)S(1)}, u32[]{:S(2)}, u32[]{:S(2)}) collective-permute-start(s32[64]{0:T(128)S(1)} %get-tuple-element.63), channel_id=1, source_target_pairs={{0,1},{1,2},{2,3},{3,4},{4,5},{5,6},{6,7},{7,8},{8,9},{9,10},{10,1... | collective-permute-start | bytes 776 | tf_op jit(solution)/shard_map/ppermute | solution.py:25
  21.2 2.1 tile.8
  23.3 3.7 copy.28.cos_ref
  28.0 2.1 tile.20
  30.0 3.5 copy.29.sin_ref
  33.7 44.8 %all-gather.3.cloned.1.call-done = bf16[6400,384]{1,0:T(8,128)(2,1)} async-done(((bf16[200,384]{1,0:T(8,128)(2,1)}), bf16[6400,384]{1,0:T(8,128)(2,1)}) %all-gather.3.cloned.1.call-update) | async-done | bytes 4915216 | tf_op jit(solution)/shard_map/all_gather | solution.py:490
  78.5 1.4 slice.98
  79.9 4.6 slice.97
  85.3 1.5 copy.40
  86.8 5.8 %copy.44 = bf16[2,384,2304]{2,1,0:T(8,128)(2,1)} copy(bf16[2,384,2304]{1,2,0:T(8,128)(2,1)} %bitcast.95) | data formatting | bytes 7077888 | tf_op jit(solution)/shard_map/tn,dnr->tdr/dot_general | solution.py:509
  93.1 1.1 copy-done.23
  94.3 8.3 %convolution_bitcast_fusion.1.qkv_ref = f32[1024,2304]{1,0:T(8,128)} fusion(bf16[2,2304,384]{2,1,0:T(8,128)(2,1)} %bitcast.96, bf16[128,2,8,384]{3,2,1,0:T(8,128)(2,1)S(1)} %bitcast.124), kind=kOutput, calls=%fused_computation.4 | convolution fusion | flops 3623878656 | bytes 14548992 | tf_op jit(solution)/shard_map/tdr,dnr->tn/dot_general | solution.py:505
  102.6 9.3 %shard_map.161 = (bf16[1024,768]{1,0:T(8,128)(2,1)}, bf16[1024,1536]{1,0:T(8,128)(2,1)}) custom-call(f32[1024,2304]{1,0:T(8,128)} %convolution_bitcast_fusion.1.qkv_ref, f32[1024,768]{1,0:T(8,128)} %copy.28.cos_ref, f32[1024,768]{1,0:T(8,128)} %copy.29.sin_ref), custom_call_target="tpu_custom_call" | custom-call | tf_op jit(solution)/shard_map/pallas_call | solution.py:461
  111.9 1.4 copy-done
  113.3 25.0 %shard_map.162 = (bf16[1024,768]{1,0:T(8,128)(2,1)S(1)}, bf16[64,1536]{1,0:T(8,128)(2,1)S(1)}, bf16[64,1536]{1,0:T(8,128)(2,1)S(1)}) custom-call(bf16[1024,768]{1,0:T(8,128)(2,1)S(1)} %copy-done, bf16[1024,1536]{1,0:T(8,128)(2,1)} %get-tuple-element.28.kv_ref, s32[1024,1]{1,0:T(8,128)S(1)} %copy.30.tq_ref, s32[1,1152]{1,0:T(1,128)S(1)} %reshape.170.tk_ref), custom_call_target="tpu_custom_call" | custom-call | tf_op jit(solution)/shard_map/pallas_call | solution.py:379
  138.4 3.1 convert_add_fusion
  141.5 6.2 %all-gather.5.cloned.1.call-done = bf16[7168,384]{1,0:T(8,128)(2,1)} async-done(((bf16[224,384]{1,0:T(8,128)(2,1)}), bf16[7168,384]{1,0:T(8,128)(2,1)}) %all-gather.5.cloned.1.call-update) | async-done | bytes 5505040 | tf_op jit(solution)/shard_map/all_gather | solution.py:490
  148.5 2.9 slice.81
  151.4 4.2 slice.78
  155.6 2.1 reduce_sum.92
  157.8 2.4 multiply_reduce_fusion.2
  160.2 4.8 %reshape_reshape.9 = bf16[2,768,576]{2,1,0:T(8,128)(2,1)} reshape(bf16[2,16,72,384]{3,2,1,0:T(8,128)(2,1)} %slice.81) | data formatting | bytes 3538944 | tf_op jit(solution)/shard_map/reshape;reshape | solution.py:566
  165.0 5.8 %copy.38 = bf16[2,384,2304]{2,1,0:T(8,128)(2,1)} copy(bf16[2,384,2304]{1,2,0:T(8,128)(2,1)} %bitcast.93) | data formatting | bytes 7077888 | tf_op jit(solution)/shard_map/tn,dnr->tdr/dot_general | solution.py:509
  170.8 6.6 %fusion.27 = f32[2,576,1024]{2,1,0:T(8,128)} fusion(bf16[2,768,576]{2,1,0:T(8,128)(2,1)} %reshape_reshape.9, bf16[1024,768]{1,0:T(8,128)(2,1)} %param.19), kind=kOutput, calls=%fused_computation.56 | convolution fusion | flops 1811939328 | bytes 8060928 | tf_op jit(solution)/shard_map/tn,dnr->tdr/dot_general | solution.py:509
  177.4 6.3 %copy.36 = f32[1024,1152]{1,0:T(8,128)} copy(f32[1024,1152]{0,1:T(8,128)} %bitcast.109) | data formatting | bytes 9437184 | tf_op jit(solution)/shard_map/reshape | solution.py:510
  183.7 2.5 multiply_convert_fusion.1
  186.2 6.5 %convolution_bitcast_fusion = f32[1024,2304]{1,0:T(8,128)S(1)} fusion(bf16[2,2304,384]{2,1,0:T(8,128)(2,1)} %bitcast.94, bf16[128,2,8,384]{3,2,1,0:T(8,128)(2,1)S(1)} %bitcast.125), kind=kOutput, calls=%fused_computation.3 | convolution fusion | flops 3623878656 | bytes 14548992 | tf_op jit(solution)/shard_map/tdr,dnr->tn/dot_general | solution.py:505
  192.7 11.1 %fusion.29 = (f32[1024,1152]{1,0:T(8,128)}, f32[1024,1152]{1,0:T(8,128)S(1)}) fusion(f32[1024,1152]{1,0:T(8,128)S(1)} %bitcast.92, f32[1024,2304]{1,0:T(8,128)S(1)} %convolution_bitcast_fusion), kind=kLoop, calls=%fused_computation.60 | loop fusion | flops 76677120 | bytes 18874368 | tf_op jit(solution)/shard_map/transpose(jvp())/mul | solution.py:80
  203.8 4.0 multiply_add_fusion
  207.8 9.1 %multiply_reduce_fusion = (f32[768]{0:T(1024)S(1)}, f32[1024]{0:T(1024)S(1)}, f32[1024]{0:T(1024)S(1)}, f32[1024,768]{1,0:T(8,128)S(1)}) fusion(f32[1024,768]{1,0:T(8,128)S(1)} %copy-done.4, f32[1024]{0:T(1024)S(1)} %add_rsqrt_fusion, f32[1024]{0:T(1024)S(1)} %broadcast_multiply_fusion.4, f32[768]{0:T(1024)S(1)} %reshape.190, ...), kind=kOutput, calls=%fused_computation.41 | convolution fusion | flops 3634885888 | bytes 19290112 | tf_op jit(solution)/shard_map/tn,dnr->tdr/dot_general | solution.py:509
  216.9 1.7 multiply_add_fusion.1
  218.6 2.1 fusion.42
  220.7 2.0 fusion.40
  222.7 2.7 convolution_bitcast_fusion.2
  225.4 2.4 convolution_bitcast_fusion.3
  227.8 1.4 convolution_convert_fusion.do_ref
  229.3 58.2 %shard_map.163 = (f32[1024,768]{1,0:T(8,128)}, f32[1024,1536]{1,0:T(8,128)}) custom-call(bf16[1024,768]{1,0:T(8,128)(2,1)S(1)} %copy-done.1, bf16[1024,1536]{1,0:T(8,128)(2,1)} %get-tuple-element.28.kv_ref, bf16[64,1536]{1,0:T(8,128)(2,1)S(1)} %get-tuple-element.32.lo_ref, bf16[64,1536]{1,0:T(8,128)(2,1)S(1)} %get-tuple-element.33.hi_ref, ...), custom_call_target="tpu_custom_call" | custom-call | tf_op jit(solution)/shard_map/pallas_call | solution.py:398
  287.5 10.0 %shard_map.164 = bf16[1024,2304]{1,0:T(8,128)(2,1)} custom-call(f32[1024,768]{1,0:T(8,128)} %get-tuple-element.34.dq_ref, f32[1024,1536]{1,0:T(8,128)} %get-tuple-element.35.dkv_ref, f32[1024,768]{1,0:T(8,128)} %copy.28.cos_ref, f32[1024,768]{1,0:T(8,128)} %copy.29.sin_ref), custom_call_target="tpu_custom_call" | custom-call | tf_op jit(solution)/shard_map/pallas_call | solution.py:475
  297.6 7.0 %fusion.32 = f32[2304,384]{1,0:T(8,128)} fusion(bf16[1024,2304]{1,0:T(8,128)(2,1)} %shard_map.164, bf16[1024,768]{1,0:T(8,128)(2,1)S(1)} %copy-done.24), kind=kOutput, calls=%fused_computation.63 | convolution fusion | flops 1811939328 | bytes 9043968 | tf_op jit(solution)/shard_map/dot_general | solution.py:516
  304.6 4.5 fusion.36
  309.1 4.5 fusion.38
  313.6 4.6 fusion.34
  318.8 1.9 copy.49
  320.7 2.4 reshape_reshape.11
  323.1 2.2 copy.46
  325.3 2.4 reshape_reshape.10
  327.8 9.3 %fusion.18 = (f32[768]{0:T(1024)S(1)}, f32[1024]{0:T(1024)S(1)}, f32[1024]{0:T(1024)S(1)}, f32[1024,768]{1,0:T(8,128)}) fusion(bf16[1024,768]{1,0:T(8,128)(2,1)S(1)} %copy-done.8, f32[1024]{0:T(1024)S(1)} %add_rsqrt_fusion.1, f32[1024]{0:T(1024)S(1)} %broadcast_multiply_fusion.5, f32[768]{0:T(1024)S(1)} %reshape.189, bf16[1024,2304]{1,0:T(8,128)(2,1)} %shard_map.164, ...), kind=kOutput, calls=%fused_computation.37 | convolution fusion | flops 3630953728 | bytes 12998656 | tf_op jit(solution)/shard_map/tn,dnr->tdr/dot_general | solution.py:509
  337.3 1.5 constant_dynamic-update-slice_fusion.9
  339.9 1.1 copy-done.11
  341.2 1.8 copy-done.18
  343.4 1.6 copy-done.17
  345.4 1.1 copy-done.10
  346.7 1.8 copy-done.16
  348.9 7.2 %pad_maximum_fusion = f32[2,6656,384]{2,1,0:T(8,128)} fusion(f32[1,6656,384]{2,1,0:T(8,128)S(1)} %bitcast.98, f32[1,6656,384]{2,1,0:T(8,128)S(1)} %bitcast.97), kind=kLoop, calls=%fused_computation | loop fusion | flops 5111808 | bytes 40894464 | tf_op jit(solution)/shard_map/stack | solution.py:602
  356.1 4.4 copy.33
  360.5 4.7 %fusion.17 = f32[1024,768]{1,0:T(8,128)} fusion(f32[1024,768]{1,0:T(8,128)S(1)} %copy-done.3, bf16[1024,768]{1,0:T(8,128)(2,1)} %param.10, f32[1024,768]{1,0:T(8,128)} %get-tuple-element.68, f32[1024]{0:T(1024)S(1)} %broadcast_multiply_fusion, f32[1024]{0:T(1024)S(1)} %broadcast_multiply_fusion.1, f32[768]{0:T(1024)S(1)} %reshape.189, ...), kind=kLoop, calls=%fused_computation.36 | loop fusion | flops 7077888 | bytes 11029504 | tf_op jit(solution)/shard_map/add | solution.py:592
  365.7 1.4 copy-done.20
  367.0 1.1 copy-done.21
  368.1 3.5 fusion.20
  371.6 13.3 %reduce-scatter.2.cloned.1.call-done = f32[1,6656,384]{2,1,0:T(8,128)} async-done(((f32[2,6656,384]{2,1,0:T(8,128)}), f32[1,6656,384]{2,1,0:T(8,128)}) %reduce-scatter.2.cloned.1.call-update) | async-done | bytes 10223632 | tf_op jit(solution)/shard_map/reduce_scatter | solution.py:624
  384.9 64.0 %shard_map.165 = f32[416,384]{1,0:T(8,128)S(1)} custom-call(f32[16,416,384]{2,1,0:T(8,128)} %bitcast.101), custom_call_target="tpu_custom_call" | custom-call | tf_op jit(solution)/shard_map/pallas_call | solution.py:210
  (124 shorter events, 14.0 us)
Async XLA Ops:
  7.2 71.3 %all-gather.3.cloned.1.call-start = ((), (), s32[]{:S(2)}) async-start(), calls=%async_computation.1 | async-start | bytes 5068800 | tf_op jit(solution)/shard_map/all_gather | solution.py:490
  9.5 138.2 %all-gather.5.cloned.1.call-start = ((), (), s32[]{:S(2)}) async-start(), calls=%async_computation.2 | async-start | bytes 5677056 | tf_op jit(solution)/shard_map/all_gather | solution.py:490
  12.8 372.1 %reduce-scatter.2.cloned.1.call-start = ((), (), s32[]{:S(2)}) async-start(), calls=%async_computation.3 | async-start | bytes 30670848 | tf_op jit(solution)/shard_map/reduce_scatter | solution.py:624
  13.7 20.0 %collective-permute-start.1 = (s32[64]{0:T(128)S(1)}, s32[64]{0:T(128)S(1)}, u32[]{:S(2)}, u32[]{:S(2)}) collective-permute-start(s32[64]{0:T(128)S(1)} %get-tuple-element.62), channel_id=1, source_target_pairs={{1,0},{2,1},{3,2},{4,3},{5,4},{6,5},{7,6},{8,7},{9,8},{10,9},{11,1... | collective-permute-start | bytes 776 | tf_op jit(solution)/shard_map/ppermute | solution.py:26
  14.9 18.7 %collective-permute-start = (s32[64]{0:T(128)S(1)}, s32[64]{0:T(128)S(1)}, u32[]{:S(2)}, u32[]{:S(2)}) collective-permute-start(s32[64]{0:T(128)S(1)} %get-tuple-element.63), channel_id=1, source_target_pairs={{0,1},{1,2},{2,3},{3,4},{4,5},{5,6},{6,7},{7,8},{8,9},{9,10},{10,1... | collective-permute-start | bytes 776 | tf_op jit(solution)/shard_map/ppermute | solution.py:25
  23.3 3.7 copy-start.6
  79.9 5.4 %copy-start.14 = (bf16[2,16,48,384]{3,2,1,0:T(8,128)(2,1)}, bf16[2,16,48,384]{3,2,1,0:T(8,128)(2,1)S(1)}, u32[]{:S(2)}) copy-start(bf16[2,16,48,384]{3,2,1,0:T(8,128)(2,1)S(1)} %slice.98) | copy-start | bytes 3538948
  93.1 1.1 copy-start.23
  111.9 1.4 copy-start
  113.3 25.0 %copy-start.7 = (bf16[1024,768]{1,0:T(8,128)(2,1)S(1)}, bf16[1024,768]{1,0:T(8,128)(2,1)}, u32[]{:S(2)}) copy-start(bf16[1024,768]{1,0:T(8,128)(2,1)} %param.10) | copy-start | bytes 4718596
  113.3 25.0 %copy-start.15 = (bf16[2,16,48,384]{3,2,1,0:T(8,128)(2,1)S(1)}, bf16[2,16,48,384]{3,2,1,0:T(8,128)(2,1)}, u32[]{:S(2)}) copy-start(bf16[2,16,48,384]{3,2,1,0:T(8,128)(2,1)} %copy-done.14) | copy-start | bytes 3538948
  183.7 9.0 %slice-start = ((s8[4718592]{0:T(1024)(128)(4,1)}), s8[4194304]{0:T(1024)(128)(4,1)S(1)}, s32[]{:S(2)}) async-start(s8[4718592]{0:T(1024)(128)(4,1)} %bitcast.91), calls=%async_computation.4 | async-start | bytes 8388608
  186.2 6.5 %copy-start.25 = (bf16[1024,768]{1,0:T(8,128)(2,1)}, bf16[1024,768]{1,0:T(8,128)(2,1)S(1)}, u32[]{:S(2)}) copy-start(bf16[1024,768]{1,0:T(8,128)(2,1)S(1)} %multiply_convert_fusion.1) | copy-start | bytes 4718596
  186.2 6.5 %slice-start.1 = ((s8[4718592]{0:T(1024)(128)(4,1)}), s8[524288]{0:T(1024)(128)(4,1)S(1)}, s32[]{:S(2)}) async-start(s8[4718592]{0:T(1024)(128)(4,1)} %bitcast.91), calls=%async_computation.5 | async-start | bytes 1048576
  203.8 4.0 copy-start.4
  207.8 17.6 %copy-start.9 = (bf16[1024,1152]{1,0:T(8,128)(2,1)}, bf16[1024,1152]{1,0:T(8,128)(2,1)S(1)}, u32[]{:S(2)}) copy-start(bf16[1024,1152]{1,0:T(8,128)(2,1)S(1)} %get-tuple-element.55) | copy-start | bytes 7077892
  207.8 9.1 %copy-start.22 = (bf16[1024,768]{1,0:T(8,128)(2,1)S(1)}, bf16[1024,768]{1,0:T(8,128)(2,1)}, u32[]{:S(2)}) copy-start(bf16[1024,768]{1,0:T(8,128)(2,1)} %param.19) | copy-start | bytes 4718596
  218.6 9.2 %copy-start.2 = (f32[1024,768]{1,0:T(8,128)}, f32[1024,768]{1,0:T(8,128)S(1)}, u32[]{:S(2)}) copy-start(f32[1024,768]{1,0:T(8,128)S(1)} %multiply_add_fusion.1) | copy-start | bytes 9437188
  225.4 2.4 copy-start.27
  227.8 1.5 copy-start.1
  287.5 10.0 %copy-start.24 = (bf16[1024,768]{1,0:T(8,128)(2,1)S(1)}, bf16[1024,768]{1,0:T(8,128)(2,1)}, u32[]{:S(2)}) copy-start(bf16[1024,768]{1,0:T(8,128)(2,1)} %copy-done.23) | copy-start | bytes 4718596
  297.5 7.1 %copy-start.12 = (bf16[1024,2304]{1,0:T(8,128)(2,1)S(1)}, bf16[1024,2304]{1,0:T(8,128)(2,1)}, u32[]{:S(2)}) copy-start(bf16[1024,2304]{1,0:T(8,128)(2,1)} %shard_map.164) | copy-start | bytes 14155780
  297.5 11.5 %slice-start.2 = ((s8[4718592]{0:T(1024)(128)(4,1)}), s8[4194304]{0:T(1024)(128)(4,1)S(1)}, s32[]{:S(2)}) async-start(s8[4718592]{0:T(1024)(128)(4,1)} %bitcast.105), calls=%async_computation.6 | async-start | bytes 8388608
  297.5 11.5 %slice-start.4 = ((s8[4718592]{0:T(1024)(128)(4,1)}), s8[4194304]{0:T(1024)(128)(4,1)S(1)}, s32[]{:S(2)}) async-start(s8[4718592]{0:T(1024)(128)(4,1)} %bitcast.112), calls=%async_computation.8 | async-start | bytes 8388608
  304.6 4.5 slice-start.3
  304.6 4.5 slice-start.5
  304.6 4.5 copy-start.26
  323.1 4.7 %copy-start.8 = (bf16[1024,768]{1,0:T(8,128)(2,1)S(1)}, bf16[1024,768]{1,0:T(8,128)(2,1)}, u32[]{:S(2)}) copy-start(bf16[1024,768]{1,0:T(8,128)(2,1)} %param.10) | copy-start | bytes 4718596
  327.8 9.4 %copy-start.28 = (f32[16,1,384]{2,1,0:T(1,128)S(1)}, f32[16,1,384]{2,1,0:T(1,128)}, u32[]{:S(2)}) copy-start(f32[16,1,384]{2,1,0:T(1,128)} %broadcast_in_dim.17) | copy-start | bytes 73732
  327.8 11.0 %copy-start.13 = (f32[768,384]{1,0:T(8,128)S(1)}, f32[768,384]{1,0:T(8,128)}, u32[]{:S(2)}) copy-start(f32[768,384]{1,0:T(8,128)} %fusion.42) | copy-start | bytes 3538948
  337.2 2.4 copy-start.19
  339.5 1.5 copy-start.11
  341.0 2.0 copy-start.18
  343.0 2.0 copy-start.17
  345.0 1.5 copy-start.10
  346.5 2.0 copy-start.16
  356.1 4.4 copy-start.3
  360.5 5.1 %copy-start.5 = (f32[1024,768]{1,0:T(8,128)S(1)}, f32[1024,768]{1,0:T(8,128)}, u32[]{:S(2)}) copy-start(f32[1024,768]{1,0:T(8,128)} %convert_add_fusion) | copy-start | bytes 9437188
  360.5 6.5 %copy-start.20 = (bf16[1024,1152]{0,1:T(8,128)(2,1)S(1)}, bf16[1024,1152]{0,1:T(8,128)(2,1)}, u32[]{:S(2)}) copy-start(bf16[1024,1152]{0,1:T(8,128)(2,1)} %copy.33) | copy-start | bytes 7077892
  360.5 7.6 %copy-start.21 = (bf16[2,768,576]{2,1,0:T(8,128)(2,1)S(1)}, bf16[2,768,576]{2,1,0:T(8,128)(2,1)}, u32[]{:S(2)}) copy-start(bf16[2,768,576]{2,1,0:T(8,128)(2,1)} %reshape_reshape.9) | copy-start | bytes 5308420
Sparse Core Ops, SparseCore 0:
  11.4 67.0 all-gather.2
  82.0 65.6 all-gather.4
  356.2 28.6 reduce-scatter.1
